TPU v7x, 32 devices: a whole 2x2x4 slice. The times are simulated.
32 devices in a mesh: replica: 2 (over core), shard: 16 (over z, y, x).
Axes of the slice: x: 2, y: 2, z: 4, core: 2. Of those that a mesh axis runs over, the one named last changes fastest.
Arguments:
- inputs: bfloat16 [32768, 768], P(('replica', 'shard')), may hold values from -6 to 6
- cotangent: bfloat16 [32768, 768], P(('replica', 'shard')), may hold values from -6 to 6
- block_ids: int32 [32, 1024], P(('replica', 'shard')), may hold values from 0 to 3, never falling along the last dimension, each value on 1 to 512 neighbouring positions
- buckets: int32 [2047], replicated, may hold values from 0 to 31
- early_gain: float32 [768], replicated, may hold values from 0.25 to 1.75
- query_weight: bfloat16 [768, 768], P('shard'), may hold values from -0.109375 to 0.109375
- key_weight: bfloat16 [768, 768], P('shard'), may hold values from -0.109375 to 0.109375
- value_weight: bfloat16 [768, 768], P('shard'), may hold values from -0.21875 to 0.21875
- mixing_weight: bfloat16 [768, 768], P('shard'), may hold values from -0.875 to 0.875
- relative_table: float32 [32, 12], replicated, may hold values from -4 to 4
- later_gain: float32 [768], replicated, may hold values from 0.25 to 1.75
- up_weight: bfloat16 [768, 3072], P('shard'), may hold values from -0.21875 to 0.21875
- down_weight: bfloat16 [3072, 768], P('shard'), may hold values from -0.109375 to 0.109375
Outputs:
- layer_output: bfloat16 [32768, 768], P(('replica', 'shard'))
- input_gradient: bfloat16 [32768, 768], P(('replica', 'shard'))
- early_gradient: float32 [768], replicated
- query_gradient: float32 [768, 768], P('shard')
- key_gradient: float32 [768, 768], P('shard')
- value_gradient: float32 [768, 768], P('shard')
- mixing_gradient: float32 [768, 768], P('shard')
- table_gradient: float32 [32, 12], replicated
- later_gradient: float32 [768], replicated
- up_gradient: float32 [768, 3072], P('shard')
- down_gradient: float32 [3072, 768], P('shard')
Inputs may be any that keep to these rules, and one draw needn't show every extreme that they name: `block_ids`: along the positions of each sequence the passage numbers never fall; a passage holds at most 512 tokens.
All inputs are finite; a program needn't handle non-finite values.
Results may differ from a plain program's by a relative error of at most 0.019.
Values may be sent and summed in bfloat16 or wider, within the bound.
No kernel may reach another device: no remote copies, remote signals or barrier semaphores. Data moves between devices by JAX's collectives and lax.ppermute only.
A program may use at most 192 MiB of HBM per device.

v0:
```python
import jax
import jax.numpy as jnp
from jax import lax
from jax.sharding import PartitionSpec as P

HEADS = 12
HEAD_DIM = 64
BUCKETS = 32
LEN = 1024
QBLOCK = 512
SEQ_DEV = 1


EPS = 1e-06
HIGH = lax.Precision.HIGHEST
NEG = -1e30


def smooth_gate(v):
    return jax.nn.gelu(v, approximate=True)


def product(left, right):
    return jnp.dot(left, right, preferred_element_type=jnp.float32)


def left_product(left, right):
    return lax.dot_general(
        left, right, (((0,), (0,)), ((), ())), preferred_element_type=jnp.float32
    )


def right_product(left, right):
    return lax.dot_general(
        left, right, (((1,), (1,)), ((), ())), preferred_element_type=jnp.float32
    )


def rms_forward(values, gain):
    scale = lax.rsqrt(jnp.mean(values * values, axis=1, keepdims=True) + EPS)
    return (scale, (values * scale * gain).astype(jnp.bfloat16))


def rms_backward(values, scale, gain, upstream):
    gain_part = jnp.sum(upstream * values * scale, axis=0)
    scaled = upstream * gain
    inner = jnp.mean(scaled * values, axis=1, keepdims=True)
    return (scale * (scaled - values * scale * scale * inner), gain_part)


def toeplitz(segment, rows, cols):
    spread = jnp.broadcast_to(segment[None, :], (rows, cols + rows - 1)).reshape(-1)
    spread = jnp.concatenate([spread, jnp.zeros((rows,), spread.dtype)])
    return spread.reshape(rows, cols + rows)[:, :cols][::-1]


def diagonal_sums(matrix):
    rows, cols = matrix.shape
    padded = jnp.concatenate([matrix[::-1], jnp.zeros((rows, rows), matrix.dtype)], axis=1).reshape(
        -1
    )
    return padded[: rows * (cols + rows - 1)].reshape(rows, cols + rows - 1).sum(axis=0)


def split_heads(matrix):
    return (
        matrix.reshape(SEQ_DEV, LEN, HEADS, HEAD_DIM)
        .transpose(0, 2, 1, 3)
        .reshape(SEQ_DEV * HEADS, LEN, HEAD_DIM)
    )


def merge_heads(stacked):
    return (
        stacked.reshape(SEQ_DEV, HEADS, LEN, HEAD_DIM)
        .transpose(0, 2, 1, 3)
        .reshape(SEQ_DEV * LEN, HEADS * HEAD_DIM)
    )


def score_block(query_block, key_rows, ids, bias_row, start):
    raw = right_product(query_block, key_rows)
    segment = lax.slice_in_dim(bias_row, LEN - start - QBLOCK, 2 * LEN - start - 1)
    raw = raw + toeplitz(segment, QBLOCK, LEN)
    allowed = ids[None, :] <= lax.slice_in_dim(ids, start, start + QBLOCK)[:, None]
    return jnp.where(allowed, raw, NEG)


def head_forward(item):
    query_rows, key_rows, value_rows, ids, bias_row = item
    outcome = []
    log_parts = []
    for start in range(0, LEN, QBLOCK):
        query_block = lax.slice_in_dim(query_rows, start, start + QBLOCK)
        scores = score_block(query_block, key_rows, ids, bias_row, start)
        peak = jnp.max(scores, axis=1, keepdims=True)
        weights = jnp.exp(scores - peak)
        total = jnp.sum(weights, axis=1, keepdims=True)
        probs = (weights / total).astype(jnp.bfloat16)
        outcome.append(product(probs, value_rows))
        log_parts.append((peak + jnp.log(total))[:, 0])
    return (
        jnp.concatenate(outcome, axis=0).astype(jnp.bfloat16),
        jnp.concatenate(log_parts, axis=0),
    )


def head_backward(item):
    query_rows, key_rows, value_rows, ids, bias_row, log_row, grad_rows = item
    key_total = jnp.zeros((LEN, HEAD_DIM), jnp.float32)
    value_total = jnp.zeros((LEN, HEAD_DIM), jnp.float32)
    bias_total = jnp.zeros((2 * LEN - 1,), jnp.float32)
    query_parts = []
    for start in range(0, LEN, QBLOCK):
        query_block = lax.slice_in_dim(query_rows, start, start + QBLOCK)
        scores = score_block(query_block, key_rows, ids, bias_row, start)
        probs = jnp.exp(scores - lax.slice_in_dim(log_row, start, start + QBLOCK)[:, None])
        grad_block = lax.slice_in_dim(grad_rows, start, start + QBLOCK)
        value_total = value_total + left_product(probs.astype(jnp.bfloat16), grad_block)
        probs_grad = right_product(grad_block, value_rows)
        inner = jnp.sum(probs * probs_grad, axis=1, keepdims=True)
        scores_grad = probs * (probs_grad - inner)
        bias_total = bias_total.at[LEN - start - QBLOCK : 2 * LEN - start - 1].add(
            diagonal_sums(scores_grad)
        )
        scores_low = scores_grad.astype(jnp.bfloat16)
        query_parts.append(product(scores_low, key_rows))
        key_total = key_total + left_product(scores_low, query_block)
    query_grad = jnp.concatenate(query_parts, axis=0).astype(jnp.bfloat16)
    return (
        query_grad,
        key_total.astype(jnp.bfloat16),
        value_total.astype(jnp.bfloat16),
        bias_total,
    )


def body(
    inputs,
    cotangent,
    block_ids,
    buckets,
    early_gain,
    query_weight,
    key_weight,
    value_weight,
    mixing_weight,
    relative_table,
    later_gain,
    up_weight,
    down_weight,
):
    values = inputs.astype(jnp.float32)
    query_full, key_full, value_full, mixing_full = (
        lax.all_gather(query_weight, "shard", axis=0, tiled=True),
        lax.all_gather(key_weight, "shard", axis=0, tiled=True),
        lax.all_gather(value_weight, "shard", axis=0, tiled=True),
        lax.all_gather(mixing_weight, "shard", axis=0, tiled=True),
    )
    up_full, down_full = (
        lax.all_gather(up_weight, "shard", axis=0, tiled=True),
        lax.all_gather(down_weight, "shard", axis=0, tiled=True),
    )
    early_scale, normed = rms_forward(values, early_gain)
    queries = product(normed, query_full).astype(jnp.bfloat16)
    key_rows = product(normed, key_full).astype(jnp.bfloat16)
    value_rows = product(normed, value_full).astype(jnp.bfloat16)
    onehot = (buckets[:, None] == jnp.arange(BUCKETS, dtype=jnp.int32)[None, :]).astype(jnp.float32)
    bias_table = jnp.dot(onehot, relative_table, precision=HIGH).T
    bias_rows = jnp.tile(bias_table, (SEQ_DEV, 1))
    id_rows = jnp.repeat(block_ids, HEADS, axis=0)
    query_heads = split_heads(queries)
    key_heads = split_heads(key_rows)
    value_heads = split_heads(value_rows)
    attended_heads, log_sums = lax.map(
        head_forward, (query_heads, key_heads, value_heads, id_rows, bias_rows)
    )
    attended = merge_heads(attended_heads)
    state = values + product(attended, mixing_full)
    later_scale, later_normed = rms_forward(state, later_gain)
    pre_act = product(later_normed, up_full)
    gate_values, gate_pull = jax.vjp(smooth_gate, pre_act)
    activated = gate_values.astype(jnp.bfloat16)
    layer_output = (state + product(activated, down_full)).astype(jnp.bfloat16)
    query_full, key_full, value_full, mixing_full = (
        lax.all_gather(query_weight, "shard", axis=0, tiled=True),
        lax.all_gather(key_weight, "shard", axis=0, tiled=True),
        lax.all_gather(value_weight, "shard", axis=0, tiled=True),
        lax.all_gather(mixing_weight, "shard", axis=0, tiled=True),
    )
    up_full, down_full = (
        lax.all_gather(up_weight, "shard", axis=0, tiled=True),
        lax.all_gather(down_weight, "shard", axis=0, tiled=True),
    )
    down_grad = left_product(activated, cotangent)
    pre_grad = gate_pull(right_product(cotangent, down_full))[0].astype(jnp.bfloat16)
    up_grad = left_product(later_normed, pre_grad)
    later_normed_grad = right_product(pre_grad, up_full)
    state_part, later_part = rms_backward(state, later_scale, later_gain, later_normed_grad)
    state_grad = cotangent.astype(jnp.float32) + state_part
    branch_grad = state_grad.astype(jnp.bfloat16)
    mixing_grad = left_product(attended, branch_grad)
    attended_grad = right_product(branch_grad, mixing_full).astype(jnp.bfloat16)
    query_heads_grad, key_heads_grad, value_heads_grad, bias_grads = lax.map(
        head_backward,
        (
            query_heads,
            key_heads,
            value_heads,
            id_rows,
            bias_rows,
            log_sums,
            split_heads(attended_grad),
        ),
    )
    query_low = merge_heads(query_heads_grad)
    key_low = merge_heads(key_heads_grad)
    value_low = merge_heads(value_heads_grad)
    query_grad = left_product(normed, query_low)
    key_grad = left_product(normed, key_low)
    value_grad = left_product(normed, value_low)
    normed_grad = (
        right_product(query_low, query_full)
        + right_product(key_low, key_full)
        + right_product(value_low, value_full)
    )
    input_part, early_part = rms_backward(values, early_scale, early_gain, normed_grad)
    input_gradient = (state_grad + input_part).astype(jnp.bfloat16)
    bias_sum = bias_grads.reshape(SEQ_DEV, HEADS, 2 * LEN - 1).sum(axis=0)
    table_part = lax.dot_general(onehot, bias_sum, (((0,), (1,)), ((), ())), precision=HIGH)
    early_total, later_total, table_total = lax.psum(
        (early_part, later_part, table_part), ("replica", "shard")
    )
    shares = (
        lax.psum_scatter(
            query_grad.astype(jnp.bfloat16), "shard", scatter_dimension=0, tiled=True
        ).astype(jnp.float32),
        lax.psum_scatter(
            key_grad.astype(jnp.bfloat16), "shard", scatter_dimension=0, tiled=True
        ).astype(jnp.float32),
        lax.psum_scatter(
            value_grad.astype(jnp.bfloat16), "shard", scatter_dimension=0, tiled=True
        ).astype(jnp.float32),
        lax.psum_scatter(
            mixing_grad.astype(jnp.bfloat16), "shard", scatter_dimension=0, tiled=True
        ).astype(jnp.float32),
        lax.psum_scatter(
            up_grad.astype(jnp.bfloat16), "shard", scatter_dimension=0, tiled=True
        ).astype(jnp.float32),
        lax.psum_scatter(
            down_grad.astype(jnp.bfloat16), "shard", scatter_dimension=0, tiled=True
        ).astype(jnp.float32),
    )
    results = (
        lax.psum(shares[0].astype(jnp.bfloat16), "replica").astype(jnp.float32),
        lax.psum(shares[1].astype(jnp.bfloat16), "replica").astype(jnp.float32),
        lax.psum(shares[2].astype(jnp.bfloat16), "replica").astype(jnp.float32),
        lax.psum(shares[3].astype(jnp.bfloat16), "replica").astype(jnp.float32),
        lax.psum(shares[4].astype(jnp.bfloat16), "replica").astype(jnp.float32),
        lax.psum(shares[5].astype(jnp.bfloat16), "replica").astype(jnp.float32),
    )
    return (
        layer_output,
        input_gradient,
        early_total,
        results[0],
        results[1],
        results[2],
        results[3],
        table_total,
        later_total,
        results[4],
        results[5],
    )


def solution(mesh):
    placed = (
        P(("replica", "shard"), None),
        P(("replica", "shard"), None),
        P(("replica", "shard"), None),
        P(),
        P(),
        P("shard", None),
        P("shard", None),
        P("shard", None),
        P("shard", None),
        P(),
        P(),
        P("shard", None),
        P("shard", None),
    )
    return jax.shard_map(
        body,
        mesh=mesh,
        in_specs=placed,
        out_specs=(
            P(("replica", "shard"), None),
            P(("replica", "shard"), None),
            P(),
            P("shard", None),
            P("shard", None),
            P("shard", None),
            P("shard", None),
            P(),
            P(),
            P("shard", None),
            P("shard", None),
        ),
        check_vma=False,
    )
```

profile of v0, /device:TPU:0, one launch (start us, length us, event | category | flops | bytes accessed | tf_op | source)
XLA Modules:
  0.0 3452.6 jit_solution(9849391561784496931)
XLA Ops:
  15.9 53.8 %all-gather.9.cloned.1.call-done = bf16[768,768]{1,0:T(8,128)(2,1)} async-done(((bf16[48,768]{1,0:T(8,128)(2,1)}), bf16[768,768]{1,0:T(8,128)(2,1)}) %all-gather.9.cloned.1.call-update) | async-done | bytes 1179664 | tf_op jit(solution)/shard_map/all_gather | solution.py:156
  75.3 52.2 %all-gather.11.cloned.1.call-done = bf16[768,768]{1,0:T(8,128)(2,1)} async-done(((bf16[48,768]{1,0:T(8,128)(2,1)}), bf16[768,768]{1,0:T(8,128)(2,1)}) %all-gather.11.cloned.1.call-update) | async-done | bytes 1179664 | tf_op jit(solution)/shard_map/all_gather | solution.py:157
  133.2 52.2 %all-gather.7.cloned.1.call-done = bf16[768,768]{1,0:T(8,128)(2,1)} async-done(((bf16[48,768]{1,0:T(8,128)(2,1)}), bf16[768,768]{1,0:T(8,128)(2,1)}) %all-gather.7.cloned.1.call-update) | async-done | bytes 1179664 | tf_op jit(solution)/shard_map/all_gather | solution.py:155
  192.3 681.8 %while.33 = (s32[]{:T(128)}, bf16[12,1024,64]{1,2,0:T(8,128)(2,1)}, f32[12,1024]{1,0:T(8,128)}, s32[12,1024]{1,0:T(8,128)S(1)}, bf16[12,1024,64]{2,1,0:T(8,128)(...) while((s32[]{:T(128)}, bf16[12,1024,64]{1,2,0:T(8,128)(2,1)}, ...), condition=%wide.region_6.7_spmd, body=%wide.region_1.6_spmd.sunk | while | flops 278200320 | bytes 81496744 | solution.py:175
  928.8 1791.7 %while.34 = (s32[]{:T(128)}, bf16[12,1024,64]{1,2,0:T(8,128)(2,1)}, bf16[12,1024,64]{1,2,0:T(8,128)(2,1)}, bf16[12,1024,64]{1,2,0:T(8,128)(2,1)}, f32[12,2047]{1...) while((s32[]{:T(128)}, bf16[12,1024,64]{1,2,0:T(8,128)(2,1)}, ...), condition=%wide.region_14.15_spmd, body=%wide.region_9.14_spmd.sunk | while | flops 684782080 | bytes 199512368 | solution.py:204
  953.8 16.7 rev.42
  1022.8 16.7 rev.43
  1103.1 16.7 rev.42
  1172.1 16.7 rev.43
  1252.4 16.7 rev.42
  1321.3 16.7 rev.43
  1401.7 16.7 rev.42
  1470.6 16.7 rev.43
  1550.9 16.7 rev.42
  1619.8 16.7 rev.43
  1700.2 16.7 rev.42
  1769.1 16.7 rev.43
  1849.5 16.7 rev.42
  1918.4 16.7 rev.43
  1998.7 16.7 rev.42
  2067.7 16.7 rev.43
  2148.0 16.7 rev.42
  2297.3 16.7 rev.42
  2446.5 16.7 rev.42
  2515.4 16.7 rev.43
  2595.8 16.7 rev.42
  2778.1 70.6 %reduce-scatter.7.cloned.1.call-done = bf16[48,768]{1,0:T(8,128)(2,1)} async-done(((bf16[768,768]{1,0:T(8,128)(2,1)}), bf16[48,768]{1,0:T(8,128)(2,1)}) %reduce-scatter.7.cloned.1.call-update) | async-done | bytes 73744 | tf_op jit(solution)/shard_map/reduce_scatter | solution.py:235
  2848.8 128.2 %reduce-scatter.9.cloned.1.call-done = bf16[48,768]{1,0:T(8,128)(2,1)} async-done(((bf16[768,768]{1,0:T(8,128)(2,1)}), bf16[48,768]{1,0:T(8,128)(2,1)}) %reduce-scatter.9.cloned.1.call-update) | async-done | bytes 73744 | tf_op jit(solution)/shard_map/reduce_scatter | solution.py:238
  2977.0 128.1 %reduce-scatter.11.cloned.1.call-done = bf16[48,768]{1,0:T(8,128)(2,1)} async-done(((bf16[768,768]{1,0:T(8,128)(2,1)}), bf16[48,768]{1,0:T(8,128)(2,1)}) %reduce-scatter.11.cloned.1.call-update) | async-done | bytes 73744 | tf_op jit(solution)/shard_map/reduce_scatter | solution.py:241
  3105.1 142.1 %reduce-scatter.15.cloned.1.call-done = bf16[48,3072]{1,0:T(8,128)(2,1)} async-done(((bf16[768,3072]{1,0:T(8,128)(2,1)}), bf16[48,3072]{1,0:T(8,128)(2,1)}) %reduce-scatter.15.cloned.1.call-update) | async-done | bytes 294928 | tf_op jit(solution)/shard_map/reduce_scatter | solution.py:247
  3247.2 142.6 %reduce-scatter.17.cloned.1.call-done = bf16[192,768]{1,0:T(8,128)(2,1)} async-done(((bf16[3072,768]{1,0:T(8,128)(2,1)}), bf16[192,768]{1,0:T(8,128)(2,1)}) %reduce-scatter.17.cloned.1.call-update) | async-done | bytes 294928 | tf_op jit(solution)/shard_map/reduce_scatter | solution.py:250
  3395.7 40.1 %all-reduce.7 = (f32[768]{0:T(1024)}, f32[32,12]{0,1:T(8,128)}, f32[768]{0:T(1024)}) all-reduce(f32[768]{0:T(1024)S(1)} %get-tuple-element.294, f32[32,12]{0,1:T(8,128)S(1)} %fusion.75, f32[768]{0:T(1024)S(1)} %copy-done.26), channel_id=1, replica_groups=mesh['replica'=2,'shard'=16] {'replica','shard'}, use_global_device_ids=true, to_apply=%region_17.18 | all-reduce | flops 1920 | bytes 15360 | tf_op jit(solution)/shard_map/psum | solution.py:231
  (1072 shorter events, 2274.8 us)
Async XLA Ops:
  7.2 62.5 %all-gather.9.cloned.1.call-start = ((), (), s32[]{:S(2)}) async-start(), calls=%async_computation.7 | async-start | bytes 1253376 | tf_op jit(solution)/shard_map/all_gather | solution.py:156
  7.9 119.6 %all-gather.11.cloned.1.call-start = ((), (), s32[]{:S(2)}) async-start(), calls=%async_computation.8 | async-start | bytes 1253376 | tf_op jit(solution)/shard_map/all_gather | solution.py:157
  8.7 176.7 %all-gather.7.cloned.1.call-start = ((), (), s32[]{:S(2)}) async-start(), calls=%async_computation.6 | async-start | bytes 1253376 | tf_op jit(solution)/shard_map/all_gather | solution.py:155
  9.4 864.7 %all-gather.13.cloned.1.call-start = ((), (), s32[]{:S(2)}) async-start(), calls=%async_computation.9 | async-start | bytes 1253376 | tf_op jit(solution)/shard_map/all_gather | solution.py:158
  10.0 868.0 %all-gather.15.cloned.1.call-start = ((), (), s32[]{:S(2)}) async-start(), calls=%async_computation.10 | async-start | bytes 5013504 | tf_op jit(solution)/shard_map/all_gather | solution.py:161
  10.6 879.1 %all-gather.17.cloned.1.call-start = ((), (), s32[]{:S(2)}) async-start(), calls=%async_computation.11 | async-start | bytes 5013504 | tf_op jit(solution)/shard_map/all_gather | solution.py:162
  11.2 2767.0 %reduce-scatter.13.cloned.1.call-start = ((), (), s32[]{:S(2)}) async-start(), calls=%async_computation.15 | async-start | bytes 1253376 | tf_op jit(solution)/shard_map/reduce_scatter | solution.py:244
  13.0 172.4 %copy-start.7 = (bf16[1024,768]{0,1:T(8,128)(2,1)}, bf16[1024,768]{0,1:T(8,128)(2,1)S(1)}, u32[]{:S(2)}) copy-start(bf16[1024,768]{0,1:T(8,128)(2,1)S(1)} %copy.38) | copy-start | bytes 4718596
  13.0 56.7 %copy-start.23 = (f32[768]{0:T(1024)S(1)}, f32[768]{0:T(1024)}, u32[]{:S(2)}) copy-start(f32[768]{0:T(1024)} %param.25) | copy-start | bytes 9220
  13.4 172.0 %copy-start.21 = (f32[1024]{0:T(1024)}, f32[1024]{0:T(1024)S(1)}, u32[]{:S(2)}) copy-start(f32[1024]{0:T(1024)S(1)} %add_rsqrt_fusion.1) | copy-start | bytes 12292
  878.0 33.3 copy-start.17
  916.7 1932.1 %reduce-scatter.7.cloned.1.call-start = ((), (), s32[]{:S(2)}) async-start(), calls=%async_computation.12 | async-start | bytes 1253376 | tf_op jit(solution)/shard_map/reduce_scatter | solution.py:235
  928.8 1791.7 %copy-start.22 = (f32[1024]{0:T(1024)S(1)}, f32[1024]{0:T(1024)}, u32[]{:S(2)}) copy-start(f32[1024]{0:T(1024)} %copy-done.21) | copy-start | bytes 12292
  928.8 1791.7 %copy-start.24 = (f32[768]{0:T(1024)S(1)}, f32[768]{0:T(1024)}, u32[]{:S(2)}) copy-start(f32[768]{0:T(1024)} %param.25) | copy-start | bytes 9220
  931.4 39.1 %copy-start.6 = (f32[512,1024]{1,0:T(8,128)}, f32[512,1024]{1,0:T(8,128)S(1)}, u32[]{:S(2)}) copy-start(f32[512,1024]{1,0:T(8,128)S(1)} %fusion.161) | copy-start | bytes 6291460 | tf_op jit(solution)/shard_map/while
  1080.9 39.0 %copy-start.6 = (f32[512,1024]{1,0:T(8,128)}, f32[512,1024]{1,0:T(8,128)S(1)}, u32[]{:S(2)}) copy-start(f32[512,1024]{1,0:T(8,128)S(1)} %fusion.161) | copy-start | bytes 6291460 | tf_op jit(solution)/shard_map/while
  1230.1 39.0 %copy-start.6 = (f32[512,1024]{1,0:T(8,128)}, f32[512,1024]{1,0:T(8,128)S(1)}, u32[]{:S(2)}) copy-start(f32[512,1024]{1,0:T(8,128)S(1)} %fusion.161) | copy-start | bytes 6291460 | tf_op jit(solution)/shard_map/while
  1379.4 39.0 %copy-start.6 = (f32[512,1024]{1,0:T(8,128)}, f32[512,1024]{1,0:T(8,128)S(1)}, u32[]{:S(2)}) copy-start(f32[512,1024]{1,0:T(8,128)S(1)} %fusion.161) | copy-start | bytes 6291460 | tf_op jit(solution)/shard_map/while
  1528.6 39.0 %copy-start.6 = (f32[512,1024]{1,0:T(8,128)}, f32[512,1024]{1,0:T(8,128)S(1)}, u32[]{:S(2)}) copy-start(f32[512,1024]{1,0:T(8,128)S(1)} %fusion.161) | copy-start | bytes 6291460 | tf_op jit(solution)/shard_map/while
  1677.9 39.0 %copy-start.6 = (f32[512,1024]{1,0:T(8,128)}, f32[512,1024]{1,0:T(8,128)S(1)}, u32[]{:S(2)}) copy-start(f32[512,1024]{1,0:T(8,128)S(1)} %fusion.161) | copy-start | bytes 6291460 | tf_op jit(solution)/shard_map/while
  1827.2 39.0 %copy-start.6 = (f32[512,1024]{1,0:T(8,128)}, f32[512,1024]{1,0:T(8,128)S(1)}, u32[]{:S(2)}) copy-start(f32[512,1024]{1,0:T(8,128)S(1)} %fusion.161) | copy-start | bytes 6291460 | tf_op jit(solution)/shard_map/while
  1976.4 39.0 %copy-start.6 = (f32[512,1024]{1,0:T(8,128)}, f32[512,1024]{1,0:T(8,128)S(1)}, u32[]{:S(2)}) copy-start(f32[512,1024]{1,0:T(8,128)S(1)} %fusion.161) | copy-start | bytes 6291460 | tf_op jit(solution)/shard_map/while
  2125.7 39.0 %copy-start.6 = (f32[512,1024]{1,0:T(8,128)}, f32[512,1024]{1,0:T(8,128)S(1)}, u32[]{:S(2)}) copy-start(f32[512,1024]{1,0:T(8,128)S(1)} %fusion.161) | copy-start | bytes 6291460 | tf_op jit(solution)/shard_map/while
  2275.0 39.0 %copy-start.6 = (f32[512,1024]{1,0:T(8,128)}, f32[512,1024]{1,0:T(8,128)S(1)}, u32[]{:S(2)}) copy-start(f32[512,1024]{1,0:T(8,128)S(1)} %fusion.161) | copy-start | bytes 6291460 | tf_op jit(solution)/shard_map/while
  2424.2 39.0 %copy-start.6 = (f32[512,1024]{1,0:T(8,128)}, f32[512,1024]{1,0:T(8,128)S(1)}, u32[]{:S(2)}) copy-start(f32[512,1024]{1,0:T(8,128)S(1)} %fusion.161) | copy-start | bytes 6291460 | tf_op jit(solution)/shard_map/while
  2573.5 39.0 %copy-start.6 = (f32[512,1024]{1,0:T(8,128)}, f32[512,1024]{1,0:T(8,128)S(1)}, u32[]{:S(2)}) copy-start(f32[512,1024]{1,0:T(8,128)S(1)} %fusion.161) | copy-start | bytes 6291460 | tf_op jit(solution)/shard_map/while
  2725.0 251.9 %reduce-scatter.9.cloned.1.call-start = ((), (), s32[]{:S(2)}) async-start(), calls=%async_computation.13 | async-start | bytes 1253376 | tf_op jit(solution)/shard_map/reduce_scatter | solution.py:238
  2729.1 375.9 %reduce-scatter.11.cloned.1.call-start = ((), (), s32[]{:S(2)}) async-start(), calls=%async_computation.14 | async-start | bytes 1253376 | tf_op jit(solution)/shard_map/reduce_scatter | solution.py:241
  2731.7 515.4 %reduce-scatter.15.cloned.1.call-start = ((), (), s32[]{:S(2)}) async-start(), calls=%async_computation.16 | async-start | bytes 5013504 | tf_op jit(solution)/shard_map/reduce_scatter | solution.py:247
  2741.4 648.3 %reduce-scatter.17.cloned.1.call-start = ((), (), s32[]{:S(2)}) async-start(), calls=%async_computation.17 | async-start | bytes 5013504 | tf_op jit(solution)/shard_map/reduce_scatter | solution.py:250
  2753.6 682.2 %all-reduce.11.cloned.1.call-start = ((), (), s32[]{:S(2)}) async-start(), calls=%async_computation.18 | async-start | bytes 1769472 | tf_op jit(solution)/shard_map/psum | solution.py:255
  3389.8 55.9 %copy-start.1 = (f32[32,12]{0,1:T(8,128)S(1)}, f32[32,12]{0,1:T(8,128)}, u32[]{:S(2)}) copy-start(f32[32,12]{0,1:T(8,128)} %param.30) | copy-start | bytes 4612
  (80 other events, 295.6 us)
Sparse Core Ops, SparseCore 0:
  10.8 58.8 all-gather.8
  72.5 54.9 all-gather.10
  130.3 54.9 all-gather.6
  188.0 55.0 all-gather.12
  245.8 79.3 all-gather.14
  327.9 79.0 all-gather.16
  916.8 123.5 reduce-scatter.12
  2725.1 123.5 reduce-scatter.6
  2853.5 123.3 reduce-scatter.8
  2981.6 123.4 reduce-scatter.10
  3110.2 136.8 reduce-scatter.14
  3253.0 136.6 reduce-scatter.16
  3392.5 18.5 all-reduce.10
where the time goes:
time: 3520 us; the launch traced here: 3450 us
  local copies, waits for them, and re-layouts  2050 us (58%)
  waiting for transfers between devices  774 us (22%)
  matrix products  437 us (12%)
  other arithmetic  131 us (4%)
  blocking collectives  40.1 us (1%)
    rev x48, local copies, waits for them, and re-layouts, toeplitz(): return spread.reshape(rows, cols + rows)[:, :cols][::-1]  691 us
    rev x24, local copies, waits for them, and re-layouts, diagonal_sums(): matrix[::-1]  289 us
    reshape x48, local copies, waits for them, and re-layouts, toeplitz(): jnp.broadcast_to(segment[None, :], (rows, cols + rows - 1)).reshape(-1)  231 us
    dot_general x78, matrix products, right_product(): lax.dot_general(left, right, (((1,), (1,)), ((), ())), preferred_element_...  209 us
    reshape x48, local copies, waits for them, and re-layouts, toeplitz(): return spread.reshape(rows, cols + rows)[:, :cols][::-1]  165 us
    reduce_scatter x1, waiting for transfers between devices, body(): lax.psum_scatter(down_grad.astype(jnp.bfloat16), 'shard', scatter_dimensi...  143 us
    reduce_scatter x1, waiting for transfers between devices, body(): lax.psum_scatter(up_grad.astype(jnp.bfloat16), 'shard', scatter_dimension...  142 us
    concatenate x48, local copies, waits for them, and re-layouts, toeplitz(): spread = jnp.concatenate([spread, jnp.zeros((rows,), spread.dtype)])  138 us
  transfers between devices with their start and end apart: 13, of which 8 were waited for; matrix products, arithmetic and copies ran while one was open for 74% of the time, Pallas kernels for 0%

commit v1 on v0

v1 whole, which is shorter than its diff:
```python
import functools
import jax
import jax.numpy as jnp
from jax import lax
from jax.experimental import pallas as pl
from jax.experimental.pallas import tpu as pltpu
from jax.sharding import PartitionSpec as P

HEAD_DIM = 64
SLAB = 128
TILE = 256
NEG = -1e30


def nt(left, right):
    return lax.dot_general(left, right, (((1,), (1,)), ((), ())), preferred_element_type=jnp.float32)


def nn(left, right):
    return lax.dot_general(left, right, (((1,), (0,)), ((), ())), preferred_element_type=jnp.float32)


def tn(left, right):
    return lax.dot_general(left, right, (((0,), (0,)), ((), ())), preferred_element_type=jnp.float32)


def skew_kernel(rows_ref, out_ref):
    width = rows_ref.shape[-1]
    keep = out_ref.shape[-1]
    for k in range(rows_ref.shape[0]):
        spread = jnp.broadcast_to(rows_ref[k], (SLAB, width))
        moved = pltpu.roll(spread, width - SLAB + 1, 1, stride=1, stride_axis=0)
        out_ref[k] = moved[:, :keep]


def skew(rows, length):
    count, width = rows.shape
    keep = 2 * length - SLAB
    return pl.pallas_call(
        skew_kernel,
        grid=(count // 2,),
        in_specs=[pl.BlockSpec((2, 1, width), lambda i: (i, 0, 0))],
        out_specs=pl.BlockSpec((2, SLAB, keep), lambda i: (i, 0, 0)),
        out_shape=jax.ShapeDtypeStruct((count, SLAB, keep), jnp.float32),
        compiler_params=pltpu.CompilerParams(vmem_limit_bytes=32 << 20),
    )(rows.reshape(count, 1, width))


def bias_tile(table_ref, k, offset):
    return jnp.concatenate(
        [
            table_ref[k, :, pl.ds(offset, TILE)],
            table_ref[k, :, pl.ds(offset - SLAB, TILE)],
        ],
        axis=0,
    )


def forward_kernel(counts_ref, q_ref, k_ref, v_ref, ends_ref, table_ref, out_ref, log_ref):
    length = q_ref.shape[0]
    tiles = length // TILE
    low = lax.broadcasted_iota(jnp.int32, (TILE, 2 * HEAD_DIM), 1) < HEAD_DIM

    def block(i, n):
        first = pl.multiple_of(i * TILE, TILE)
        query = q_ref[pl.ds(first, TILE), :]
        ends = ends_ref[pl.ds(first, TILE), :]
        keys = k_ref[0 : n * TILE, :]
        values = v_ref[0 : n * TILE, :]
        columns = lax.broadcasted_iota(jnp.int32, (TILE, n * TILE), 1)
        allowed = columns < ends
        outs = []
        zero = jnp.zeros_like(query)
        for k in range(2):
            mine = jnp.where(low, query, zero) if k == 0 else jnp.where(low, zero, query)
            offset = pl.multiple_of((tiles - 1 - i) * TILE + SLAB, SLAB)
            bias = jnp.concatenate(
                [
                    table_ref[k, :, pl.ds(offset, n * TILE)],
                    table_ref[k, :, pl.ds(pl.multiple_of(offset - SLAB, SLAB), n * TILE)],
                ],
                axis=0,
            )
            scores = jnp.where(allowed, nt(mine, keys) + bias, NEG)
            peak = jnp.max(scores, axis=1, keepdims=True)
            weights = jnp.exp(scores - peak)
            total = jnp.sum(weights, axis=1, keepdims=True)
            scaled = nn(weights.astype(jnp.bfloat16), values)
            outs.append(scaled / total)
            logs = jnp.broadcast_to(peak + jnp.log(total), (TILE, SLAB))
            log_ref[0, k : k + 1, pl.ds(first, TILE)] = logs.T[0:1, :]
        out_ref[pl.ds(first, TILE), :] = jnp.where(low, outs[0], outs[1]).astype(out_ref.dtype)

    def step(i, carry):
        count = counts_ref[i]
        for n in range(1, tiles + 1):
            @pl.when(count == n)
            def _():
                block(i, n)
        return carry

    lax.fori_loop(0, tiles, step, 0)


def attend_forward(qkv, ends, counts, table, heads, first_pair, pairs):
    length = qkv.shape[0]
    half = heads // 2
    width = 2 * HEAD_DIM
    keep = table.shape[-1]
    return pl.pallas_call(
        forward_kernel,
        grid_spec=pltpu.PrefetchScalarGridSpec(
            num_scalar_prefetch=1,
            grid=(pairs,),
            in_specs=[
                pl.BlockSpec((length, width), lambda p, c: (0, first_pair + p)),
                pl.BlockSpec((length, width), lambda p, c: (0, half + first_pair + p)),
                pl.BlockSpec((length, width), lambda p, c: (0, 2 * half + first_pair + p)),
                pl.BlockSpec((length, 1), lambda p, c: (0, 0)),
                pl.BlockSpec((2, SLAB, keep), lambda p, c: (first_pair + p, 0, 0)),
            ],
            out_specs=[
                pl.BlockSpec((length, width), lambda p, c: (0, p)),
                pl.BlockSpec((1, 2, length), lambda p, c: (p, 0, 0)),
            ],
        ),
        out_shape=[
            jax.ShapeDtypeStruct((length, pairs * width), jnp.bfloat16),
            jax.ShapeDtypeStruct((pairs, 2, length), jnp.float32),
        ],
        compiler_params=pltpu.CompilerParams(vmem_limit_bytes=48 << 20),
        cost_estimate=pl.CostEstimate(
            flops=pairs * 2 * 4 * length * length * HEAD_DIM * 2,
            bytes_accessed=pairs * (4 * length * width * 2 + 2 * SLAB * keep * 4),
            transcendentals=pairs * 2 * length * length,
        ),
    )(counts, qkv, qkv, qkv, ends, table)


def backward_kernel(
    tiles_ref, q_ref, k_ref, v_ref, out_ref, grad_ref, ends_ref, log_ref, table_ref,
    dq_ref, dk_ref, dv_ref, diag_ref,
    qm, km, gm, dq_acc, dk_acc, dv_acc, skewed, delta,
):
    length = q_ref.shape[0]
    tiles = length // TILE
    width = 2 * HEAD_DIM
    low = lax.broadcasted_iota(jnp.int32, (length, width), 1) < HEAD_DIM
    query, keys, grads = q_ref[...], k_ref[...], grad_ref[...]
    zero = jnp.zeros_like(query)
    for k in range(2):
        pick = low if k == 0 else jnp.logical_not(low)
        qm[k] = jnp.where(pick, query, zero)
        km[k] = jnp.where(pick, keys, zero)
        gm[k] = jnp.where(pick, grads, zero)
    dq_acc[...] = jnp.zeros_like(dq_acc)
    dk_acc[...] = jnp.zeros_like(dk_acc)
    dv_acc[...] = jnp.zeros_like(dv_acc)
    skewed[...] = jnp.zeros_like(skewed)
    product = grads.astype(jnp.float32) * out_ref[...].astype(jnp.float32)
    high = product.astype(jnp.bfloat16)
    rest = (product - high.astype(jnp.float32)).astype(jnp.bfloat16)
    lane = lax.broadcasted_iota(jnp.int32, (16, width), 1)
    row = lax.broadcasted_iota(jnp.int32, (16, width), 0)
    chooser = jnp.where(lane // HEAD_DIM == row, 1.0, 0.0).astype(jnp.bfloat16)
    delta[...] = nt(chooser, high) + nt(chooser, rest)

    def tile(t, carry):
        kb = tiles_ref[1 + 2 * t]
        qb = tiles_ref[2 + 2 * t]
        kf = pl.multiple_of(kb * TILE, TILE)
        qf = pl.multiple_of(qb * TILE, TILE)
        offset = pl.multiple_of((tiles - 1 + qb - kb) * TILE + SLAB, SLAB)
        before = pl.multiple_of(offset - SLAB, SLAB)
        rows = lax.broadcasted_iota(jnp.int32, (TILE, TILE), 0) + kf
        allowed = rows < ends_ref[:, pl.ds(qf, TILE)]
        q_tile = q_ref[pl.ds(qf, TILE), :]
        v_tile = v_ref[pl.ds(kf, TILE), :]
        dk_part = dk_acc[pl.ds(kf, TILE), :]
        dv_part = dv_acc[pl.ds(kf, TILE), :]
        dq_part = dq_acc[pl.ds(qf, TILE), :]
        for k in range(2):
            k_tile = km[k, pl.ds(kf, TILE), :]
            g_tile = gm[k, pl.ds(qf, TILE), :]
            bias = jnp.concatenate(
                [table_ref[k, :, pl.ds(offset, TILE)], table_ref[k, :, pl.ds(before, TILE)]], axis=0
            )
            scores = nt(k_tile, q_tile) + bias - log_ref[0, k : k + 1, pl.ds(qf, TILE)]
            probs = jnp.where(allowed, jnp.exp(scores), 0.0)
            above = nt(v_tile, g_tile) - delta[k : k + 1, pl.ds(qf, TILE)]
            grad = probs * above
            skewed[k, :, pl.ds(offset, TILE)] += grad[:SLAB]
            skewed[k, :, pl.ds(before, TILE)] += grad[SLAB:]
            probs_low = probs.astype(jnp.bfloat16)
            grad_low = grad.astype(jnp.bfloat16)
            dv_part = dv_part + nn(probs_low, g_tile)
            dk_part = dk_part + nn(grad_low, qm[k, pl.ds(qf, TILE), :])
            dq_part = dq_part + tn(grad_low, k_tile)
        dk_acc[pl.ds(kf, TILE), :] = dk_part
        dv_acc[pl.ds(kf, TILE), :] = dv_part
        dq_acc[pl.ds(qf, TILE), :] = dq_part
        return carry

    lax.fori_loop(0, tiles_ref[0], tile, 0)
    dq_ref[...] = dq_acc[...].astype(dq_ref.dtype)
    dk_ref[...] = dk_acc[...].astype(dk_ref.dtype)
    dv_ref[...] = dv_acc[...].astype(dv_ref.dtype)
    lanes = skewed.shape[-1]
    group = lax.broadcasted_iota(jnp.int32, (SLAB, lanes), 0)
    for k in range(2):
        held = skewed[k]
        shift = 1
        while shift < SLAB:
            moved = pltpu.roll(held, shift, 1)
            held = jnp.where(((SLAB - 1 - group) & shift) != 0, moved, held)
            shift *= 2
        diag_ref[0, k : k + 1, :] = jnp.sum(held, axis=0, keepdims=True)


def attend_backward(qkv, out, grad, ends, logs, tile_list, table, heads, first_pair, pairs):
    length = qkv.shape[0]
    half = heads // 2
    width = 2 * HEAD_DIM
    keep = table.shape[-1]
    lanes = 2 * length
    piece = pl.BlockSpec((length, width), lambda p, c: (0, p))
    return pl.pallas_call(
        backward_kernel,
        grid_spec=pltpu.PrefetchScalarGridSpec(
            num_scalar_prefetch=1,
            grid=(pairs,),
            in_specs=[
                pl.BlockSpec((length, width), lambda p, c: (0, first_pair + p)),
                pl.BlockSpec((length, width), lambda p, c: (0, half + first_pair + p)),
                pl.BlockSpec((length, width), lambda p, c: (0, 2 * half + first_pair + p)),
                pl.BlockSpec((length, width), lambda p, c: (0, first_pair + p)),
                pl.BlockSpec((length, width), lambda p, c: (0, first_pair + p)),
                pl.BlockSpec((1, length), lambda p, c: (0, 0)),
                pl.BlockSpec((1, 2, length), lambda p, c: (first_pair + p, 0, 0)),
                pl.BlockSpec((2, SLAB, keep), lambda p, c: (first_pair + p, 0, 0)),
            ],
            out_specs=[piece, piece, piece, pl.BlockSpec((1, 2, lanes), lambda p, c: (p, 0, 0))],
            scratch_shapes=[
                pltpu.VMEM((2, length, width), jnp.bfloat16),
                pltpu.VMEM((2, length, width), jnp.bfloat16),
                pltpu.VMEM((2, length, width), jnp.bfloat16),
                pltpu.VMEM((length, width), jnp.float32),
                pltpu.VMEM((length, width), jnp.float32),
                pltpu.VMEM((length, width), jnp.float32),
                pltpu.VMEM((2, SLAB, lanes), jnp.float32),
                pltpu.VMEM((16, length), jnp.float32),
            ],
        ),
        out_shape=[jax.ShapeDtypeStruct((length, pairs * width), jnp.bfloat16)] * 3
        + [jax.ShapeDtypeStruct((pairs, 2, lanes), jnp.float32)],
        compiler_params=pltpu.CompilerParams(vmem_limit_bytes=48 << 20),
        cost_estimate=pl.CostEstimate(
            flops=pairs * 2 * 10 * length * length * HEAD_DIM * 2,
            bytes_accessed=pairs * (8 * length * width * 2 + 2 * SLAB * keep * 4),
            transcendentals=pairs * 2 * length * length,
        ),
    )(tile_list, qkv, qkv, qkv, out, grad, ends, logs, table)


EPS = 1e-06
HIGH = lax.Precision.HIGHEST
EVERY = ("shard", "replica")


def smooth_gate(v):
    return jax.nn.gelu(v, approximate=True)


def rms_forward(values, gain):
    scale = lax.rsqrt(jnp.mean(values * values, axis=1, keepdims=True) + EPS)
    return (scale, (values * scale * gain).astype(jnp.bfloat16))


def rms_backward(values, scale, gain, upstream):
    gain_part = jnp.sum(upstream * values * scale, axis=0)
    scaled = upstream * gain
    inner = jnp.mean(scaled * values, axis=1, keepdims=True)
    return (scale * (scaled - values * scale * scale * inner), gain_part)


def gather_rows(shard_rows, copies):
    part = shard_rows.shape[0] // copies
    own = lax.dynamic_slice_in_dim(shard_rows, lax.axis_index("replica") * part, part, 0)
    return lax.all_gather(own, EVERY, axis=0, tiled=True)


def scatter_rows(partial):
    part = lax.psum_scatter(partial.astype(jnp.bfloat16), EVERY, scatter_dimension=0, tiled=True)
    return lax.all_gather(part, "replica", axis=0, tiled=True).astype(jnp.float32)


def exchange_rows(partial, copies, shards):
    rows, columns = partial.shape
    wide = columns // copies
    if copies == 2:
        me = lax.axis_index("replica")
        own = lax.dynamic_slice_in_dim(partial, me * wide, wide, 1)
        sent = lax.dynamic_slice_in_dim(partial, (1 - me) * wide, wide, 1).astype(jnp.bfloat16)
        other = lax.ppermute(sent, "replica", [(0, 1), (1, 0)])
        both = own + other.astype(jnp.float32)
    else:
        pieces = partial.astype(jnp.bfloat16).reshape(rows, copies, wide)
        both = lax.all_to_all(pieces, "replica", 1, 0).astype(jnp.float32).sum(axis=0)
    pieces = both.astype(jnp.bfloat16).reshape(shards, rows // shards, wide)
    summed = lax.all_to_all(pieces, "shard", 0, 0).astype(jnp.float32).sum(axis=0)
    return lax.all_gather(summed, "replica", axis=1, tiled=True)


def body(
    copies,
    shards,
    inputs,
    cotangent,
    block_ids,
    buckets,
    early_gain,
    query_weight,
    key_weight,
    value_weight,
    mixing_weight,
    relative_table,
    later_gain,
    up_weight,
    down_weight,
):
    length, width = inputs.shape
    bucket_count, heads = relative_table.shape
    hidden = up_weight.shape[1]
    pairs = heads // 2
    offsets = buckets.shape[0]
    qkv_weight = gather_rows(jnp.concatenate([query_weight, key_weight, value_weight], axis=1), copies)
    mixing_up = gather_rows(jnp.concatenate([mixing_weight, up_weight], axis=1), copies)
    mixing_full, up_full = mixing_up[:, :width], mixing_up[:, width:]
    down_full = gather_rows(down_weight, copies)

    ids = block_ids.reshape(length)
    ends = jnp.sum((ids[None, :] <= ids[:, None]).astype(jnp.int32), axis=1)
    tiles = length // TILE
    last = ends.reshape(tiles, TILE)[:, TILE - 1]
    counts = (last + TILE - 1) // TILE
    key_block = jnp.repeat(jnp.arange(tiles, dtype=jnp.int32), tiles)
    query_block = jnp.tile(jnp.arange(tiles, dtype=jnp.int32), tiles)
    active = (key_block.reshape(tiles, tiles) * TILE < last[None, :]).reshape(-1)
    slot = jnp.arange(tiles * tiles, dtype=jnp.int32)
    place = jnp.sum((slot[None, :] < slot[:, None]) & active[None, :], axis=1, dtype=jnp.int32)
    hit = ((place[None, :] == slot[:, None]) & active[None, :]).astype(jnp.int32)
    listed = jnp.stack(
        [jnp.sum(hit * key_block[None, :], axis=1), jnp.sum(hit * query_block[None, :], axis=1)], axis=1
    ).reshape(-1)
    tile_list = jnp.concatenate([jnp.sum(active.astype(jnp.int32))[None], listed])

    onehot = (buckets[:, None] == jnp.arange(bucket_count, dtype=jnp.int32)[None, :]).astype(jnp.float32)
    bias_rows = jnp.dot(onehot, relative_table, precision=HIGH).T
    spare = ((0, 0), (0, 2 * length - offsets))
    forward_table = skew(jnp.pad(bias_rows, spare), length)
    backward_table = skew(jnp.pad(bias_rows[:, ::-1], spare), length)

    values = inputs.astype(jnp.float32)
    early_scale, normed = rms_forward(values, early_gain)
    qkv = nn(normed, qkv_weight).astype(jnp.bfloat16)
    attended, logs = attend_forward(qkv, ends[:, None], counts, forward_table, heads, 0, pairs)
    state = values + nn(attended, mixing_full)
    later_scale, later_normed = rms_forward(state, later_gain)
    pre_act = nn(later_normed, up_full)
    gate_values, gate_pull = jax.vjp(smooth_gate, pre_act)
    activated = gate_values.astype(jnp.bfloat16)
    layer_output = (state + nn(activated, down_full)).astype(jnp.bfloat16)
    down_share = scatter_rows(tn(activated, cotangent))
    pre_grad = gate_pull(nt(cotangent, down_full))[0].astype(jnp.bfloat16)
    up_grad = tn(later_normed, pre_grad)
    later_normed_grad = nt(pre_grad, up_full)
    state_part, later_part = rms_backward(state, later_scale, later_gain, later_normed_grad)
    state_grad = cotangent.astype(jnp.float32) + state_part
    branch_grad = state_grad.astype(jnp.bfloat16)
    mixing_grad = tn(attended, branch_grad)
    mixing_up_share = scatter_rows(jnp.concatenate([mixing_grad, up_grad], axis=1))
    attended_grad = nt(branch_grad, mixing_full).astype(jnp.bfloat16)
    query_low, key_low, value_low, diagonals = attend_backward(
        qkv, attended, attended_grad, ends[None, :], logs, tile_list, backward_table, heads, 0, pairs
    )
    low = jnp.concatenate([query_low, key_low, value_low], axis=1)
    qkv_share = exchange_rows(tn(normed, low), copies, shards)
    normed_grad = nt(low, qkv_weight)
    input_part, early_part = rms_backward(values, early_scale, early_gain, normed_grad)
    input_gradient = (state_grad + input_part).astype(jnp.bfloat16)
    diagonals = diagonals.reshape(heads, 2 * length)[:, :offsets][:, ::-1]
    table_part = lax.dot_general(onehot, diagonals, (((0,), (1,)), ((), ())), precision=HIGH)
    early_total, later_total, table_total = lax.psum(
        (early_part, later_part, table_part), ("replica", "shard")
    )
    return (
        layer_output,
        input_gradient,
        early_total,
        qkv_share[:, :width],
        qkv_share[:, width : 2 * width],
        qkv_share[:, 2 * width :],
        mixing_up_share[:, :width],
        table_total,
        later_total,
        mixing_up_share[:, width:],
        down_share,
    )


def solution(mesh):
    rows = P(("replica", "shard"), None)
    split = P("shard", None)
    same = P()
    return jax.shard_map(
        functools.partial(body, mesh.shape["replica"], mesh.shape["shard"]),
        mesh=mesh,
        in_specs=(rows, rows, rows, same, same, split, split, split, split, same, same, split, split),
        out_specs=(rows, rows, same, split, split, split, split, same, same, split, split),
        check_vma=False,
    )
```

time: 3520 us -> 501 us (0.14); the launches traced: 3450 us -> 493 us
  local copies, waits for them, and re-layouts: 2050 us -> 41.5 us
  waiting for transfers between devices: 774 us -> 119 us
  matrix products: 437 us -> 89.8 us
  Pallas kernels: 0 us -> 137 us
  other arithmetic: 131 us -> 19.2 us
    rev x72 -> x0, local copies, waits for them, and re-layouts: 980 us -> none  [the longest x48 691 us: toeplitz(): return spread.reshape(rows, cols + rows)[:, :cols][::-1]]
    reshape x149 -> x6, local copies, waits for them, and re-layouts: 606 us -> 0.36 us  [the longest x3 0.19 us: skew(): rows.reshape(count, 1, width)]
    reduce_scatter x6 -> x2, waiting for transfers between devices: 612 us -> 12.1 us  [scatter_rows(): lax.psum_scatter(partial.astype(jnp.bfloat16), EVERY, scatter_dimension=0...]
    dot_general x188 -> x14, matrix products: 437 us -> 89.8 us  [the longest x4 38.5 us: nt(): lax.dot_general(left, right, (((1,), (1,)), ((), ())), preferred_element_...]
    concatenate x72 -> x1, local copies, waits for them, and re-layouts: 205 us -> 1.34 us  [body(): low = jnp.concatenate([query_low, key_low, value_low], axis=1)]
    pallas_call x0 -> x4, Pallas kernels: none -> 137 us  [the longest x1 96.3 us: attend_backward(): pl.pallas_call(backward_kernel, grid_spec=pltpu.PrefetchScalarGridSpec(nu...]
    slice x120 -> x4, local copies, waits for them, and re-layouts: 128 us -> 2.48 us  [the longest x1 0.85 us: body(): mixing_up_share[:, width:]]
    broadcast_in_dim x60 -> x2, local copies, waits for them, and re-layouts: 78.4 us -> 0.23 us  [the longest x1 0.22 us: body(): ends[:, None]]
  transfers between devices with their start and end apart: 13 -> 7, of which waited for: 8 -> 4; matrix products, arithmetic and copies ran while one was open for 74% -> 26% of each run, Pallas kernels for 0% -> 28%
where the time goes in v1:
time: 501 us; the launch traced here: 493 us
  Pallas kernels  137 us (27%)
  waiting for transfers between devices  119 us (24%)
  matrix products  89.8 us (18%)
  blocking collectives  65.9 us (13%)
  local copies, waits for them, and re-layouts  41.5 us (8%)
  other arithmetic  19.2 us (4%)
  between operations  14.7 us (3%)
  starting transfers between devices  5.05 us (1%)
    all_gather x3, waiting for transfers between devices, gather_rows(): return lax.all_gather(own, EVERY, axis=0, tiled=True)  107 us
    pallas_call x1, Pallas kernels, attend_backward(): pl.pallas_call(backward_kernel, grid_spec=pltpu.PrefetchScalarGridSpec(nu...  96.3 us
    psum x1, blocking collectives, body(): lax.psum((early_part, later_part, table_part), ('replica', 'shard'))  59.3 us
    dot_general x4, matrix products, nt(): lax.dot_general(left, right, (((1,), (1,)), ((), ())), preferred_element_...  38.5 us
    pallas_call x1, Pallas kernels, attend_forward(): pl.pallas_call(forward_kernel, grid_spec=pltpu.PrefetchScalarGridSpec(num...  33.7 us
    unnamed x65, local copies, waits for them, and re-layouts  33.2 us
    dot_general x4, matrix products, nn(): lax.dot_general(left, right, (((1,), (0,)), ((), ())), preferred_element_...  27.7 us
    dot_general x4, matrix products, tn(): lax.dot_general(left, right, (((0,), (0,)), ((), ())), preferred_element_...  22 us
  transfers between devices with their start and end apart: 7, of which 4 were waited for; matrix products, arithmetic and copies ran while one was open for 26% of the time, Pallas kernels for 28%

profile of v1, /device:TPU:0, one launch (start us, length us, event | category | flops | bytes accessed | tf_op | source)
XLA Modules:
  0.0 493.0 jit_solution(12848170664894436840)
XLA Ops:
  15.0 3.7 shard_map.212.table_ref
  18.7 4.4 copy-done.2
  23.0 2.6 copy.69
  28.6 3.7 shard_map.214.table_ref
  32.3 4.2 copy-done.3
  37.7 36.7 %all-gather.4.cloned.1.call-done = bf16[768,2304]{1,0:T(8,128)(2,1)} async-done(((bf16[24,2304]{1,0:T(8,128)(2,1)}), bf16[768,2304]{1,0:T(8,128)(2,1)}) %all-gather.4.cloned.1.call-update) | async-done | bytes 3538960 | tf_op jit(solution)/shard_map/all_gather | solution.py:289
  74.4 7.8 %convolution_convert_fusion.q_ref.k_ref.v_ref = bf16[1024,2304]{1,0:T(8,128)(2,1)} fusion(bf16[768,2304]{1,0:T(8,128)(2,1)} %all-gather.4.cloned.1.call-done, bf16[1024,768]{0,1:T(8,128)(2,1)S(1)} %copy.65, f32[768]{0:T(1024)S(1)} %copy-done.18, f32[1024]{0:T(1024)S(1)} %add_rsqrt_fusion.1), kind=kOutput, calls=%fused_computation.21 | convolution fusion | flops 3629383680 | bytes 9837568 | tf_op jit(solution)/shard_map/dot_general | solution.py:20
  82.2 33.7 %shard_map.213 = (bf16[1024,768]{1,0:T(8,128)(2,1)S(1)}, f32[6,2,1024]{2,1,0:T(2,128)S(1)}) custom-call(s32[4]{0:T(128)S(1)} %and_select_fusion.counts_ref, bf16[1024,2304]{1,0:T(8,128)(2,1)} %convolution_convert_fusion.q_ref.k_ref.v_ref, bf16[1024,2304]{1,0:T(8,128)(2,1)} %convolution_convert_fusion.q_ref.k_ref.v_ref, ...), custom_call_target="tpu_custom_call" | custom-call | flops 6442450944 | bytes 18087936 | tf_op jit(solution)/shard_map/pallas_call | solution.py:110
  116.0 28.3 %all-gather.6.cloned.1.call-done = bf16[768,3840]{1,0:T(8,128)(2,1)} async-done(((bf16[24,3840]{1,0:T(8,128)(2,1)}), bf16[768,3840]{1,0:T(8,128)(2,1)}) %all-gather.6.cloned.1.call-update) | async-done | bytes 5898256 | tf_op jit(solution)/shard_map/all_gather | solution.py:289
  144.3 3.5 multiply_reduce_fusion.2
  149.5 5.3 %fusion.12 = f32[1024,3072]{1,0:T(8,128)S(1)} fusion(bf16[768,3840]{1,0:T(8,128)(2,1)S(1)} %copy-done.20, f32[1024,768]{0,1:T(8,128)S(1)} %get-tuple-element.82, f32[768]{0:T(1024)S(1)} %copy-done.19, f32[1024]{0:T(1024)S(1)} %add_rsqrt_fusion), kind=kOutput, calls=%fused_computation.27 | convolution fusion | flops 4834197504 | bytes 20455424 | tf_op jit(solution)/shard_map/dot_general | solution.py:20
  154.8 4.5 copy-done.24
  159.3 8.9 %convolution_convert_fusion.1 = bf16[3072,768]{1,0:T(8,128)(2,1)} fusion(bf16[1024,768]{1,0:T(8,128)(2,1)S(1)} %copy-done.16, f32[1024,3072]{1,0:T(8,128)S(1)} %fusion.12), kind=kOutput, calls=%fused_computation.22 | convolution fusion | flops 4862509056 | bytes 18874368 | tf_op jit(solution)/shard_map/dot_general | solution.py:24
  168.3 42.2 %all-gather.8.cloned.1.call-done = bf16[3072,768]{1,0:T(8,128)(2,1)} async-done(((bf16[96,768]{1,0:T(8,128)(2,1)}), bf16[3072,768]{1,0:T(8,128)(2,1)}) %all-gather.8.cloned.1.call-update) | async-done | bytes 4718608 | tf_op jit(solution)/shard_map/all_gather | solution.py:289
  210.4 14.2 %fusion.6 = bf16[1024,3072]{1,0:T(8,128)(2,1)S(1)} fusion(f32[1024,3072]{1,0:T(8,128)} %copy-done.24, bf16[3072,768]{1,0:T(8,128)(2,1)} %all-gather.8.cloned.1.call-done, bf16[1024,768]{1,0:T(8,128)(2,1)S(1)} %copy-done.16), kind=kOutput, calls=%fused_computation.8 | convolution fusion | flops 4894752768 | bytes 25165824 | tf_op jit(solution)/shard_map/dot_general | solution.py:16
  224.7 9.9 %multiply_reduce_fusion = (f32[768]{0:T(1024)S(1)}, f32[1024]{0:T(1024)S(1)}, f32[1024,768]{0,1:T(8,128)S(1)}) fusion(f32[1024,768]{0,1:T(8,128)S(1)} %copy-done.14, f32[1024]{0:T(1024)S(1)} %add_rsqrt_fusion, f32[768]{0:T(1024)S(1)} %copy-done.19, bf16[1024,3072]{1,0:T(8,128)(2,1)S(1)} %fusion.6, bf16[768,3840]{1,0:T(8,128)(2,1)} %all-gather.6.cloned.1.call-done), kind=kOutput, calls=%fused_computation.44 | convolution fusion | flops 4836554752 | bytes 17315840 | tf_op jit(solution)/shard_map/dot_general | solution.py:16
  240.0 5.1 %convolution_convert_fusion.3.grad_ref = bf16[1024,768]{1,0:T(8,128)(2,1)} fusion(bf16[768,3840]{1,0:T(8,128)(2,1)} %all-gather.6.cloned.1.call-done, f32[1024,768]{0,1:T(8,128)} %copy-done.8), kind=kOutput, calls=%fused_computation.51 | convolution fusion | flops 1209532416 | bytes 5898240 | tf_op jit(solution)/shard_map/dot_general | solution.py:16
  245.1 96.3 %shard_map.215 = (bf16[1024,768]{1,0:T(8,128)(2,1)S(1)}, bf16[1024,768]{1,0:T(8,128)(2,1)S(1)}, bf16[1024,768]{1,0:T(8,128)(2,1)S(1)}, f32[6,2,2048]{2,1,0:T(2,128)S(1)}) custom-call(s32[33]{0:T(128)S(1)} %pad_add_fusion.1.tiles_ref, bf16[1024,2304]{1,0:T(8,128)(2,1)} %convolution_convert_fusion.q_ref.k_ref.v_ref, ...), custom_call_target="tpu_custom_call" | custom-call | flops 16106127360 | bytes 24379392 | tf_op jit(solution)/shard_map/pallas_call | solution.py:227
  343.8 5.4 %convolution_convert_fusion.2 = bf16[768,3072]{1,0:T(8,128)(2,1)S(1)} fusion(bf16[1024,3072]{1,0:T(8,128)(2,1)S(1)} %bitcast.48, f32[1024,768]{0,1:T(8,128)S(1)} %copy-done.15, f32[768]{0:T(1024)S(1)} %copy-done.19, f32[1024]{0:T(1024)S(1)} %add_rsqrt_fusion), kind=kOutput, calls=%fused_computation.23 | convolution fusion | flops 4836556800 | bytes 14162944 | tf_op jit(solution)/shard_map/dot_general | solution.py:24
  349.2 2.9 pad_maximum_fusion
  354.9 6.3 %fusion.33 = f32[768,2304]{1,0:T(8,128)S(1)} fusion(bf16[1024,2304]{1,0:T(8,128)(2,1)} %constant_dynamic-update-slice_fusion, bf16[1024,768]{0,1:T(8,128)(2,1)S(1)} %copy-done.6, f32[768]{0:T(1024)S(1)} %copy-done.18, f32[1024]{0:T(1024)S(1)} %add_rsqrt_fusion.1), kind=kOutput, calls=%fused_computation.61 | convolution fusion | flops 3627024384 | bytes 13376512 | tf_op jit(solution)/shard_map/dot_general | solution.py:24
  361.2 2.8 copy-done.11
  366.9 9.4 %fusion.25 = (f32[768]{0:T(1024)S(1)}, f32[1024]{0:T(1024)S(1)}, f32[1024,768]{0,1:T(8,128)}) fusion(bf16[1024,768]{0,1:T(8,128)(2,1)S(1)} %copy-done.7, f32[1024]{0:T(1024)S(1)} %add_rsqrt_fusion.1, f32[768]{0:T(1024)S(1)} %copy-done.18, bf16[1024,2304]{1,0:T(8,128)(2,1)} %constant_dynamic-update-slice_fusion, ...), kind=kOutput, calls=%fused_computation.43 | convolution fusion | flops 3629381888 | bytes 12990464 | tf_op jit(solution)/shard_map/dot_general | solution.py:16
  376.3 3.1 add_convert_fusion
  379.5 4.8 all-to-all-start
  384.3 3.9 fusion.21
  389.8 11.1 %add_convert_fusion.1 = bf16[1024,768]{0,1:T(8,128)(2,1)S(1)} fusion(f32[1024,768]{0,1:T(8,128)} %copy-done.13, bf16[3072,768]{1,0:T(8,128)(2,1)} %all-gather.8.cloned.1.call-done, f32[1024,3072]{1,0:T(8,128)} %copy-done.24), kind=kOutput, calls=%fused_computation.47 | convolution fusion | flops 4861722624 | bytes 22020096 | tf_op jit(solution)/shard_map/dot_general | solution.py:20
  403.1 59.3 %all-reduce.2 = (f32[768]{0:T(1024)}, f32[32,12]{0,1:T(8,128)}, f32[768]{0:T(1024)}) all-reduce(f32[768]{0:T(1024)S(1)} %get-tuple-element.69, f32[32,12]{0,1:T(8,128)S(1)} %fusion.26, f32[768]{0:T(1024)S(1)} %get-tuple-element.67), channel_id=1, replica_groups=mesh['replica'=2,'shard'=16] {'replica','shard'}, use_global_device_ids=true, to_apply=%region_10.11 | all-reduce | flops 1920 | bytes 15360 | tf_op jit(solution)/shard_map/psum | solution.py:393
  464.2 2.1 all_gather.21
  467.1 2.2 all_gather.23
  470.1 12.1 %reduce-scatter.3.cloned.1.call-done = bf16[24,3840]{1,0:T(8,128)(2,1)} async-done(((bf16[768,3840]{1,0:T(8,128)(2,1)}), bf16[24,3840]{1,0:T(8,128)(2,1)}) %reduce-scatter.3.cloned.1.call-update) | async-done | bytes 184336 | tf_op jit(solution)/shard_map/reduce_scatter | solution.py:293
  482.3 2.3 all_gather.22
  (118 shorter events, 35.4 us)
Async XLA Ops:
  7.2 3.4 copy-start
  7.2 5.9 %copy-start.17 = (s32[1,1024]{1,0:T(1,128)S(1)}, s32[1,1024]{1,0:T(1,128)}, u32[]{:S(2)}) copy-start(s32[1,1024]{1,0:T(1,128)} %param.15) | copy-start | bytes 12292
  7.2 6.7 %copy-start.22 = (s32[2047]{0:T(1024)S(1)}, s32[2047]{0:T(1024)}, u32[]{:S(2)}) copy-start(s32[2047]{0:T(1024)} %param.16) | copy-start | bytes 24568
  7.2 6.7 %copy-start.21 = (f32[32,12]{0,1:T(8,128)S(1)}, f32[32,12]{0,1:T(8,128)}, u32[]{:S(2)}) copy-start(f32[32,12]{0,1:T(8,128)} %param.22) | copy-start | bytes 4612
  7.2 67.2 %all-gather.4.cloned.1.call-start = ((), (), s32[]{:S(2)}) async-start(), calls=%async_computation.3 | async-start | bytes 3649536 | tf_op jit(solution)/shard_map/all_gather | solution.py:289
  8.8 135.5 %all-gather.6.cloned.1.call-start = ((), (), s32[]{:S(2)}) async-start(), calls=%async_computation.4 | async-start | bytes 6082560 | tf_op jit(solution)/shard_map/all_gather | solution.py:289
  10.5 199.9 %all-gather.8.cloned.1.call-start = ((), (), s32[]{:S(2)}) async-start(), calls=%async_computation.5 | async-start | bytes 4866048 | tf_op jit(solution)/shard_map/all_gather | solution.py:289
  11.3 455.8 %reduce-scatter.5.cloned.1.call-start = ((), (), s32[]{:S(2)}) async-start(), calls=%async_computation.7 | async-start | bytes 4866048 | tf_op jit(solution)/shard_map/reduce_scatter | solution.py:293
  13.0 61.4 %copy-start.5 = (bf16[1024,768]{0,1:T(8,128)(2,1)}, bf16[1024,768]{0,1:T(8,128)(2,1)S(1)}, u32[]{:S(2)}) copy-start(bf16[1024,768]{0,1:T(8,128)(2,1)S(1)} %copy.65) | copy-start | bytes 4718596
  18.7 4.4 copy-start.2
  28.6 45.8 %copy-start.18 = (f32[768]{0:T(1024)S(1)}, f32[768]{0:T(1024)}, u32[]{:S(2)}) copy-start(f32[768]{0:T(1024)} %param.17) | copy-start | bytes 9220
  32.3 4.3 copy-start.3
  115.9 119.5 %copy-start.4 = (bf16[1024,768]{1,0:T(8,128)(2,1)}, bf16[1024,768]{1,0:T(8,128)(2,1)S(1)}, u32[]{:S(2)}) copy-start(bf16[1024,768]{1,0:T(8,128)(2,1)S(1)} %get-tuple-element.17.out_ref) | copy-start | bytes 4718596
  144.3 5.2 %copy-start.19 = (f32[768]{0:T(1024)S(1)}, f32[768]{0:T(1024)}, u32[]{:S(2)}) copy-start(f32[768]{0:T(1024)} %param.23) | copy-start | bytes 9220
  144.3 5.2 %copy-start.20 = (bf16[768,3840]{1,0:T(8,128)(2,1)S(1)}, bf16[768,3840]{1,0:T(8,128)(2,1)}, u32[]{:S(2)}) copy-start(bf16[768,3840]{1,0:T(8,128)(2,1)} %all-gather.6.cloned.1.call-done) | copy-start | bytes 17694724
  149.5 9.8 %copy-start.16 = (bf16[1024,768]{1,0:T(8,128)(2,1)S(1)}, bf16[1024,768]{1,0:T(8,128)(2,1)}, u32[]{:S(2)}) copy-start(bf16[1024,768]{1,0:T(8,128)(2,1)} %param.14) | copy-start | bytes 4718596
  154.8 4.5 copy-start.24
  168.2 314.0 %reduce-scatter.3.cloned.1.call-start = ((), (), s32[]{:S(2)}) async-start(), calls=%async_computation.6 | async-start | bytes 6082560 | tf_op jit(solution)/shard_map/reduce_scatter | solution.py:293
  210.4 14.2 %copy-start.14 = (f32[1024,768]{0,1:T(8,128)S(1)}, f32[1024,768]{0,1:T(8,128)}, u32[]{:S(2)}) copy-start(f32[1024,768]{0,1:T(8,128)} %copy-done.13) | copy-start | bytes 9437188
  224.6 9.9 %copy-start.25 = (bf16[1024,3072]{1,0:T(8,128)(2,1)}, bf16[1024,3072]{1,0:T(8,128)(2,1)S(1)}, u32[]{:S(2)}) copy-start(bf16[1024,3072]{1,0:T(8,128)(2,1)S(1)} %fusion.6) | copy-start | bytes 18874372
  224.6 9.9 %copy-start.9 = (bf16[1024,768]{0,1:T(8,128)(2,1)S(1)}, bf16[1024,768]{0,1:T(8,128)(2,1)}, u32[]{:S(2)}) copy-start(bf16[1024,768]{0,1:T(8,128)(2,1)} %copy.69) | copy-start | bytes 4718596
  240.0 102.7 %slice-start = ((s8[6291456]{0:T(1024)(128)(4,1)}), s8[4194304]{0:T(1024)(128)(4,1)S(1)}, s32[]{:S(2)}) async-start(s8[6291456]{0:T(1024)(128)(4,1)} %bitcast.47), calls=%async_computation.8 | async-start | bytes 8388608
  245.1 97.6 %slice-start.1 = ((s8[6291456]{0:T(1024)(128)(4,1)}), s8[2097152]{0:T(1024)(128)(4,1)S(1)}, s32[]{:S(2)}) async-start(s8[6291456]{0:T(1024)(128)(4,1)} %bitcast.47), calls=%async_computation.9 | async-start | bytes 4194304
  341.4 2.5 copy-start.15
  343.8 5.4 %copy-start.10 = (bf16[768,768]{1,0:T(8,128)(2,1)S(1)}, bf16[768,768]{1,0:T(8,128)(2,1)}, u32[]{:S(2)}) copy-start(bf16[768,768]{1,0:T(8,128)(2,1)} %copy.75) | copy-start | bytes 3538948
  352.2 2.7 copy-start.6
  361.2 2.8 copy-start.11
  364.0 2.9 copy-start.7
  365.4 10.9 %collective-permute-start = (bf16[768,1152]{1,0:T(8,128)(2,1)}, bf16[768,1152]{1,0:T(8,128)(2,1)}, u32[]{:S(2)}, u32[]{:S(2)}) collective-permute-start(bf16[768,1152]{1,0:T(8,128)(2,1)} %dynamic-slice_convert_fusion), channel_id=1, source_target_pairs={{0,16},{16,0},{1,17},{17,1},{2,18},{18,2},{3,19},{19,3},{4,20},{20... | collective-permute-start | bytes 5308424 | tf_op jit(solution)/shard_map/ppermute | solution.py:304
  366.9 9.4 %copy-start.12 = (f32[768,2304]{1,0:T(8,128)S(1)}, f32[768,2304]{1,0:T(8,128)}, u32[]{:S(2)}) copy-start(f32[768,2304]{1,0:T(8,128)} %copy-done.11) | copy-start | bytes 21233668
  379.5 83.0 %all-to-all-start = ((bf16[16,48,1152]{2,1,0:T(8,128)(2,1)}), bf16[16,48,1152]{2,1,0:T(8,128)(2,1)}, u32[]{:S(2)}, u32[]{:S(2)}) async-start(bf16[16,48,1152]{2,1,0:T(8,128)(2,1)} %bitcast.42), calls=%async_computation | async-start | bytes 3538944 | tf_op jit(solution)/shard_map/all_to_all | solution.py:310
  403.1 83.0 %copy-start.1 = (bf16[192,768]{1,0:T(8,128)(2,1)S(1)}, bf16[192,768]{1,0:T(8,128)(2,1)}, u32[]{:S(2)}) copy-start(bf16[192,768]{1,0:T(8,128)(2,1)} %param.25) | copy-start | bytes 884740
  (3 other events, 4.9 us)
Sparse Core Ops, SparseCore 0:
  11.5 62.8 all-gather.3
  77.9 66.3 all-gather.5
  147.8 62.6 all-gather.7
  215.8 105.8 reduce-scatter.4
  352.3 129.9 reduce-scatter.2
